TPU v7x, 32 devices: a whole 2x2x4 slice. The times are simulated.
32 devices in a mesh: row: 4 (over z), col: 8 (over y, x, core).
Axes of the slice: x: 2, y: 2, z: 4, core: 2. Of those that a mesh axis runs over, the one named last changes fastest.
Arguments:
- amplitudes: bfloat16 [512, 8, 4096], P('col', None, 'row'), may hold values from -6 to 6
- integrals: bfloat16 [32, 4096, 4096], P(None, 'row', 'col'), may hold values from -0.046875 to 0.046875
- blocks: int32 [32, 2], replicated, may hold values from 0 to 7, as said below
Outputs:
- ladder: bfloat16 [512, 8, 4096], P(('row', 'col'))
Inputs may be any that keep to these rules, and one draw needn't show every extreme that they name: No (contracted tile, output tile) pair appears twice; each of the 8 contracted tiles and each output tile appears in exactly 4 blocks.
All inputs are finite; a program needn't handle non-finite values.
Results may differ from a plain program's by a relative error of at most 0.001.
Values may be sent and summed in bfloat16 or wider, within the bound.
A program may use at most 192 MiB of HBM per device.

v0:
```python
import jax
import jax.numpy as jnp
from jax import lax
from jax.sharding import PartitionSpec as P


def contract(panel_rows, integrals, sorted_rows, sorted_blocks, per_column):
    pair_count = panel_rows.shape[0]
    tile_total = panel_rows.shape[1]
    inner_size = panel_rows.shape[2]
    outer_size = integrals.shape[2]
    columns = []
    for tile in range(tile_total):
        lower = tile * per_column
        left_rows = jnp.take(panel_rows, sorted_rows[lower : lower + per_column], axis=1)
        left_rows = left_rows.reshape(pair_count, per_column * inner_size)
        right_cols = jnp.take(integrals, sorted_blocks[lower : lower + per_column], axis=0)
        right_cols = right_cols.reshape(per_column * inner_size, outer_size)
        columns.append(jnp.dot(left_rows, right_cols, preferred_element_type=jnp.float32))
    return jnp.stack(columns, axis=1)


def on_device(amplitudes, integrals, blocks):
    tile_total = amplitudes.shape[1]
    per_column = integrals.shape[0] // tile_total
    sorted_blocks = jnp.argsort(blocks[:, 1], stable=True)
    sorted_rows = jnp.take(blocks[:, 0], sorted_blocks, axis=0)
    gathered = lax.all_gather(amplitudes, "col", axis=0, tiled=True)
    summed = lax.psum_scatter(
        contract(gathered, integrals, sorted_rows, sorted_blocks, per_column),
        "row",
        scatter_dimension=0,
        tiled=True,
    )
    ladder = lax.all_to_all(
        summed.astype(jnp.bfloat16), "col", split_axis=0, concat_axis=2, tiled=True
    )
    return ladder


def solution(mesh):
    return jax.shard_map(
        on_device,
        mesh=mesh,
        in_specs=(P("col", None, "row"), P(None, "row", "col"), P()),
        out_specs=P(("row", "col"), None, None),
        check_vma=False,
    )
```

profile of v0, /device:TPU:0, one launch (start us, length us, event | category | flops | bytes accessed | tf_op | source)
XLA Modules:
  0.0 344.8 jit_solution(5663963951102570635)
XLA Ops:
  16.8 5.3 %gather_fusion.4 = bf16[4,1024,512]{2,1,0:T(8,128)(2,1)} fusion(bf16[32,1024,512]{2,1,0:T(8,128)(2,1)} %param.8, s32[1024]{0:T(1024)S(1)} %get-tuple-element.77), kind=kCustom, calls=%fused_computation.9.clone | custom fusion | bytes 8388624 | tf_op jit(solution)/shard_map/jit(_take)/gather | solution.py:17
  27.0 5.0 %gather_fusion.8 = bf16[4,1024,512]{2,1,0:T(8,128)(2,1)} fusion(bf16[32,1024,512]{2,1,0:T(8,128)(2,1)} %param.8, s32[1024]{0:T(1024)S(1)} %get-tuple-element.75), kind=kCustom, calls=%fused_computation.11.clone | custom fusion | bytes 8388624 | tf_op jit(solution)/shard_map/jit(_take)/gather | solution.py:17
  37.0 5.0 %gather_fusion.12 = bf16[4,1024,512]{2,1,0:T(8,128)(2,1)} fusion(bf16[32,1024,512]{2,1,0:T(8,128)(2,1)} %param.8, s32[1024]{0:T(1024)S(1)} %get-tuple-element.73), kind=kCustom, calls=%fused_computation.13.clone | custom fusion | bytes 8388624 | tf_op jit(solution)/shard_map/jit(_take)/gather | solution.py:17
  42.0 5.0 %gather_fusion.14 = bf16[4,1024,512]{2,1,0:T(8,128)(2,1)} fusion(bf16[32,1024,512]{2,1,0:T(8,128)(2,1)} %param.8, s32[1024]{0:T(1024)S(1)} %get-tuple-element.72), kind=kCustom, calls=%fused_computation.14.clone | custom fusion | bytes 8388624 | tf_op jit(solution)/shard_map/jit(_take)/gather | solution.py:17
  47.0 5.1 %gather_fusion.16 = bf16[4,1024,512]{2,1,0:T(8,128)(2,1)} fusion(bf16[32,1024,512]{2,1,0:T(8,128)(2,1)} %param.8, s32[1024]{0:T(1024)S(1)} %get-tuple-element.71), kind=kCustom, calls=%fused_computation.15.clone | custom fusion | bytes 8388624 | tf_op jit(solution)/shard_map/jit(_take)/gather | solution.py:17
  52.9 13.6 %all-gather.2.cloned.1.call-done = bf16[512,8,1024]{2,0,1:T(8,128)(2,1)} async-done(((bf16[64,8,1024]{2,0,1:T(8,128)(2,1)}), bf16[512,8,1024]{2,0,1:T(8,128)(2,1)}) %all-gather.2.cloned.1.call-update) | async-done | bytes 8388624 | tf_op jit(solution)/shard_map/all_gather | solution.py:28
  66.5 6.2 %gather_fusion.1 = bf16[4,512,1024]{2,1,0:T(8,128)(2,1)} fusion(bf16[512,8,1024]{2,0,1:T(8,128)(2,1)} %all-gather.2.cloned.1.call-done, s32[1024]{0:T(1024)S(1)} %get-tuple-element.86), kind=kCustom, calls=%fused_computation.clone | custom fusion | bytes 8388624 | tf_op jit(solution)/shard_map/jit(_take)/gather | solution.py:15
  72.7 6.9 %fusion.69 = f32[512,8,512]{2,0,1:T(8,128)} fusion(bf16[4,1024,512]{2,1,0:T(8,128)(2,1)} %gather_fusion.2, pred[4]{0:T(512)(128)(4,1)S(1)} %get-tuple-element.67, bf16[4,512,1024]{2,1,0:T(8,128)(2,1)} %gather_fusion.1, pred[4]{0:T(512)(128)(4,1)S(1)} %get-tuple-element.55), kind=kOutput, calls=%fused_computation.82 | convolution fusion | flops 2151677952 | bytes 9437192 | tf_op jit(solution)/shard_map/dot_general | solution.py:19
  79.7 6.1 %gather_fusion.3 = bf16[4,512,1024]{2,1,0:T(8,128)(2,1)} fusion(bf16[512,8,1024]{2,0,1:T(8,128)(2,1)} %all-gather.2.cloned.1.call-done, s32[1024]{0:T(1024)S(1)} %get-tuple-element.85), kind=kCustom, calls=%fused_computation.2.clone | custom fusion | bytes 8388624 | tf_op jit(solution)/shard_map/jit(_take)/gather | solution.py:15
  85.8 6.8 %fusion.79 = f32[512,8,512]{2,0,1:T(8,128)} fusion(f32[512,8,512]{2,0,1:T(8,128)} %fusion.69, bf16[4,1024,512]{2,1,0:T(8,128)(2,1)} %gather_fusion.4, pred[4]{0:T(512)(128)(4,1)S(1)} %get-tuple-element.65, bf16[4,512,1024]{2,1,0:T(8,128)(2,1)} %gather_fusion.3, pred[4]{0:T(512)(128)(4,1)S(1)} %get-tuple-element.53), kind=kOutput, calls=%fused_computation.84 | convolution fusion | flops 2151677952 | bytes 9437192 | tf_op jit(solution)/shard_map/dot_general | solution.py:19
  92.6 6.1 %gather_fusion.5 = bf16[4,512,1024]{2,1,0:T(8,128)(2,1)} fusion(bf16[512,8,1024]{2,0,1:T(8,128)(2,1)} %all-gather.2.cloned.1.call-done, s32[1024]{0:T(1024)S(1)} %get-tuple-element.84), kind=kCustom, calls=%fused_computation.3.clone | custom fusion | bytes 8388624 | tf_op jit(solution)/shard_map/jit(_take)/gather | solution.py:15
  98.8 6.8 %fusion.89 = f32[512,8,512]{2,0,1:T(8,128)} fusion(f32[512,8,512]{2,0,1:T(8,128)} %fusion.79, bf16[4,1024,512]{2,1,0:T(8,128)(2,1)} %gather_fusion.6, pred[4]{0:T(512)(128)(4,1)S(1)} %get-tuple-element.63, bf16[4,512,1024]{2,1,0:T(8,128)(2,1)} %gather_fusion.5, pred[4]{0:T(512)(128)(4,1)S(1)} %get-tuple-element.51), kind=kOutput, calls=%fused_computation.86 | convolution fusion | flops 2151677952 | bytes 9437192 | tf_op jit(solution)/shard_map/dot_general | solution.py:19
  105.6 6.2 %gather_fusion.7 = bf16[4,512,1024]{2,1,0:T(8,128)(2,1)} fusion(bf16[512,8,1024]{2,0,1:T(8,128)(2,1)} %all-gather.2.cloned.1.call-done, s32[1024]{0:T(1024)S(1)} %get-tuple-element.83), kind=kCustom, calls=%fused_computation.4.clone | custom fusion | bytes 8388624 | tf_op jit(solution)/shard_map/jit(_take)/gather | solution.py:15
  111.8 6.9 %fusion.99 = f32[512,8,512]{2,0,1:T(8,128)} fusion(f32[512,8,512]{2,0,1:T(8,128)} %fusion.89, bf16[4,1024,512]{2,1,0:T(8,128)(2,1)} %gather_fusion.8, pred[4]{0:T(512)(128)(4,1)S(1)} %get-tuple-element.61, bf16[4,512,1024]{2,1,0:T(8,128)(2,1)} %gather_fusion.7, pred[4]{0:T(512)(128)(4,1)S(1)} %get-tuple-element.49), kind=kOutput, calls=%fused_computation.88 | convolution fusion | flops 2151677952 | bytes 9437192 | tf_op jit(solution)/shard_map/dot_general | solution.py:19
  118.6 6.2 %gather_fusion.9 = bf16[4,512,1024]{2,1,0:T(8,128)(2,1)} fusion(bf16[512,8,1024]{2,0,1:T(8,128)(2,1)} %all-gather.2.cloned.1.call-done, s32[1024]{0:T(1024)S(1)} %get-tuple-element.82), kind=kCustom, calls=%fused_computation.5.clone | custom fusion | bytes 8388624 | tf_op jit(solution)/shard_map/jit(_take)/gather | solution.py:15
  124.9 7.1 %fusion.109 = f32[512,8,512]{2,0,1:T(8,128)} fusion(f32[512,8,512]{2,0,1:T(8,128)} %fusion.99, bf16[4,1024,512]{2,1,0:T(8,128)(2,1)} %gather_fusion.10, pred[4]{0:T(512)(128)(4,1)S(1)} %get-tuple-element.59, bf16[4,512,1024]{2,1,0:T(8,128)(2,1)} %gather_fusion.9, pred[4]{0:T(512)(128)(4,1)S(1)} %get-tuple-element.47), kind=kOutput, calls=%fused_computation.90 | convolution fusion | flops 2151677952 | bytes 9437192 | tf_op jit(solution)/shard_map/dot_general | solution.py:19
  132.0 6.1 %gather_fusion.11 = bf16[4,512,1024]{2,1,0:T(8,128)(2,1)} fusion(bf16[512,8,1024]{2,0,1:T(8,128)(2,1)} %all-gather.2.cloned.1.call-done, s32[1024]{0:T(1024)S(1)} %get-tuple-element.81), kind=kCustom, calls=%fused_computation.6.clone | custom fusion | bytes 8388624 | tf_op jit(solution)/shard_map/jit(_take)/gather | solution.py:15
  138.1 6.9 %fusion.119 = f32[512,8,512]{2,0,1:T(8,128)} fusion(f32[512,8,512]{2,0,1:T(8,128)} %fusion.109, bf16[4,1024,512]{2,1,0:T(8,128)(2,1)} %gather_fusion.12, pred[4]{0:T(512)(128)(4,1)S(1)} %get-tuple-element.57, bf16[4,512,1024]{2,1,0:T(8,128)(2,1)} %gather_fusion.11, pred[4]{0:T(512)(128)(4,1)S(1)} %get-tuple-element.45), kind=kOutput, calls=%fused_computation.92 | convolution fusion | flops 2151677952 | bytes 9437192 | tf_op jit(solution)/shard_map/dot_general | solution.py:19
  145.0 6.2 %gather_fusion.13 = bf16[4,512,1024]{2,1,0:T(8,128)(2,1)} fusion(bf16[512,8,1024]{2,0,1:T(8,128)(2,1)} %all-gather.2.cloned.1.call-done, s32[1024]{0:T(1024)S(1)} %get-tuple-element.80), kind=kCustom, calls=%fused_computation.7.clone | custom fusion | bytes 8388624 | tf_op jit(solution)/shard_map/jit(_take)/gather | solution.py:15
  151.1 6.9 %fusion.129 = f32[512,8,512]{2,0,1:T(8,128)} fusion(f32[512,8,512]{2,0,1:T(8,128)} %fusion.119, bf16[4,1024,512]{2,1,0:T(8,128)(2,1)} %gather_fusion.14, pred[4]{0:T(512)(128)(4,1)S(1)} %get-tuple-element.69, bf16[4,512,1024]{2,1,0:T(8,128)(2,1)} %gather_fusion.13, pred[4]{0:T(512)(128)(4,1)S(1)} %get-tuple-element.43), kind=kOutput, calls=%fused_computation.94 | convolution fusion | flops 2151677952 | bytes 9437192 | tf_op jit(solution)/shard_map/dot_general | solution.py:19
  158.0 6.2 %gather_fusion.15 = bf16[4,512,1024]{2,1,0:T(8,128)(2,1)} fusion(bf16[512,8,1024]{2,0,1:T(8,128)(2,1)} %all-gather.2.cloned.1.call-done, s32[1024]{0:T(1024)S(1)} %get-tuple-element.79), kind=kCustom, calls=%fused_computation.8.clone | custom fusion | bytes 8388624 | tf_op jit(solution)/shard_map/jit(_take)/gather | solution.py:15
  164.2 6.9 %fusion.139 = f32[512,8,512]{2,0,1:T(8,128)} fusion(f32[512,8,512]{2,0,1:T(8,128)} %fusion.129, bf16[4,1024,512]{2,1,0:T(8,128)(2,1)} %gather_fusion.16, pred[4]{0:T(512)(128)(4,1)S(1)} %get-tuple-element.11, bf16[4,512,1024]{2,1,0:T(8,128)(2,1)} %gather_fusion.15, pred[4]{0:T(512)(128)(4,1)S(1)} %get-tuple-element.9), kind=kOutput, calls=%fused_computation.96 | convolution fusion | flops 2151677952 | bytes 9437192 | tf_op jit(solution)/shard_map/dot_general | solution.py:19
  171.0 144.8 %reduce-scatter.2.cloned.1.call-done = f32[128,8,512]{2,0,1:T(8,128)} async-done(((f32[512,8,512]{2,0,1:T(8,128)}), f32[128,8,512]{2,0,1:T(8,128)}) %reduce-scatter.2.cloned.1.call-update) | async-done | bytes 2097168 | tf_op jit(solution)/shard_map/reduce_scatter | solution.py:29
  318.1 18.8 %all_to_all.18 = bf16[128,8,512]{2,1,0:T(8,128)(2,1)S(1)} all-to-all(bf16[128,8,512]{2,1,0:T(8,128)(2,1)S(1)} %copy.16), channel_id=1, replica_groups=mesh['row'=4,'col'=8] {'col'}, dimensions={0} | all-to-all | bytes 2097152 | tf_op jit(solution)/shard_map/all_to_all | solution.py:35
  (28 shorter events, 24.3 us)
Async XLA Ops:
  6.5 60.0 %all-gather.2.cloned.1.call-start = ((), (), s32[]{:S(2)}) async-start(), calls=%async_computation.2 | async-start | bytes 9437184 | tf_op jit(solution)/shard_map/all_gather | solution.py:28
  9.3 306.5 %reduce-scatter.2.cloned.1.call-start = ((), (), s32[]{:S(2)}) async-start(), calls=%async_computation.3 | async-start | bytes 10485760 | tf_op jit(solution)/shard_map/reduce_scatter | solution.py:29
Sparse Core Ops, SparseCore 0:
  9.5 57.0 all-gather.1
  171.1 144.6 reduce-scatter.1
where the time goes:
time: 345 us
  waiting for transfers between devices  158 us (46%)
  local copies, waits for them, and re-layouts  95.3 us (28%)
  matrix products  55.1 us (16%)
  blocking collectives  18.8 us (5%)
  between operations  13.5 us (4%)
  other arithmetic  3.59 us (1%)
    reduce_scatter x1, waiting for transfers between devices, on_device(): lax.psum_scatter(contract(gathered, integrals, sorted_rows, sorted_blocks...  145 us
    dot_general x8, matrix products, contract(): jnp.dot(left_rows, right_cols, preferred_element_type=jnp.float32)  55.1 us
    gather x8, local copies, waits for them, and re-layouts, contract(): jnp.take(panel_rows, sorted_rows[lower:lower + per_column], axis=1)  49.3 us
    gather x8, local copies, waits for them, and re-layouts, contract(): jnp.take(integrals, sorted_blocks[lower:lower + per_column], axis=0)  40.1 us
    all_to_all x1, blocking collectives, on_device(): lax.all_to_all(summed.astype(jnp.bfloat16), 'col', split_axis=0, concat_a...  18.8 us
    all_gather x1, waiting for transfers between devices, on_device(): gathered = lax.all_gather(amplitudes, 'col', axis=0, tiled=True)  13.6 us
  transfers between devices with their start and end apart: 2, of which 2 were waited for; matrix products, arithmetic and copies ran while one was open for 13% of the time, Pallas kernels for 0%

commit v1 on v0

v1 whole, which is shorter than its diff:
```python
import functools

import jax
import jax.numpy as jnp
from jax import lax
from jax.experimental import pallas as pl
from jax.experimental.pallas import tpu as pltpu
from jax.sharding import PartitionSpec as P

MESH = pl.DeviceIdType.MESH
LAG = 2
STEPS = 32767.0


def flip(index, bit):
    return index + bit - 2 * bit * ((index // bit) % 2)


def kernel(
    sizes,
    order_ref,
    amp_ref,
    int_ref,
    out_ref,
    held_0,
    held_1,
    blocks_vmem,
    acc,
    fin,
    *rest,
):
    R, C, tiles, per = sizes
    levels = R.bit_length() - 1
    chips = C // 2
    keep = rest[0:levels]
    send_q = rest[levels : 2 * levels]
    recv_q = rest[2 * levels : 3 * levels]
    send_s = rest[3 * levels : 4 * levels]
    recv_s = rest[4 * levels : 5 * levels]
    (int_sem, own_sem, gsend, grecv, zq_send, zq_recv, zs_send, zs_recv,
     out_send, out_recv) = rest[5 * levels :]
    held = (held_0, held_1)
    chunks = 2 * tiles
    slab_rows = acc.shape[1]
    width = acc.shape[2]
    half_tiles = tiles // 2
    share = out_ref.shape[1]

    r = lax.axis_index("row")
    c = lax.axis_index("col")
    q = c // 2
    core = c % 2
    sibling = 2 * q + 1 - core

    blocks_copy = pltpu.make_async_copy(int_ref, blocks_vmem, int_sem)
    blocks_copy.start()

    barrier = pltpu.get_barrier_semaphore()
    for step in range(1, C):
        pl.semaphore_signal(
            barrier, inc=1, device_id=(r, (c + step) % C), device_id_type=MESH
        )
    for level in range(levels):
        pl.semaphore_signal(
            barrier, inc=1, device_id=(flip(r, 1 << level), c), device_id_type=MESH
        )
    pl.semaphore_wait(barrier, C - 1 + levels)

    def slot(h, v, who):
        return held[h].at[pl.ds(v * half_tiles, half_tiles), who]

    def push(h, v, who, target, number, own=False):
        source = amp_ref.at[h, pl.ds(v * half_tiles, half_tiles)] if own else slot(h, v, who)
        return pltpu.make_async_remote_copy(
            src_ref=source,
            dst_ref=slot(h, v, who),
            send_sem=gsend.at[h, v, number],
            recv_sem=grecv.at[h, v, number],
            device_id=(r, target),
            device_id_type=MESH,
        )

    def chip(k):
        there = q
        bit = 1
        while bit < chips:
            if k & bit:
                there = flip(there, bit)
            bit *= 2
        return 2 * there + core

    def to_sibling(h, v, k, own=False):
        return push(h, v, chip(k), sibling, chips + k, own)

    def same_core(h, v, k):
        return push(h, v, chip(k), chip(k), k)

    def own_copy(h):
        return pltpu.make_async_copy(
            amp_ref.at[h], held[h].at[:, c], own_sem.at[h]
        )

    relayed = chips == 4
    near = (1, 2) if relayed else tuple(range(1, chips))

    def send_own(h):
        for turn in range(2):
            for k in near:
                v = turn if k != 2 else 1 - turn
                push(h, v, c, chip(k), k, own=True).start()
        for v in range(2):
            to_sibling(h, v, 0, own=True).start()
        own_copy(h).start()

    def pass_near(h):
        for turn in range(2):
            for k in near:
                v = turn if k != 2 else 1 - turn
                same_core(h, v, k).wait_recv()
                if relayed and turn == 0:
                    push(h, v, chip(k), chip(3 - k), 3).start()
                to_sibling(h, v, k).start()

    def pass_far(h):
        if relayed:
            for v in range(2):
                same_core(h, v, 3).wait_recv()
                to_sibling(h, v, 3).start()

    def finish(h):
        own_copy(h).wait()
        for v in range(2):
            for k in range(chips):
                to_sibling(h, v, k).wait_recv()

    def finish_sends(h):
        for v in range(2):
            for number in range(1, 2 * chips):
                push(h, v, c, chip(1), number).wait_send()

    def z_copies(level, t):
        partner = (flip(r, 1 << level), c)
        return (
            pltpu.make_async_remote_copy(
                src_ref=send_q[level].at[t],
                dst_ref=recv_q[level].at[t],
                send_sem=zq_send.at[level, t],
                recv_sem=zq_recv.at[level, t],
                device_id=partner,
                device_id_type=MESH,
            ),
            pltpu.make_async_remote_copy(
                src_ref=send_s[level].at[t],
                dst_ref=recv_s[level].at[t],
                send_sem=zs_send.at[level, t],
                recv_sem=zs_recv.at[level, t],
                device_id=partner,
                device_id_type=MESH,
            ),
        )

    def exchange(level, t, get):
        bit = (r // (1 << level)) % 2
        for i in range(R >> (level + 1)):
            x = get(2 * i + 1 - bit)
            peak = jnp.maximum(jnp.max(jnp.abs(x), axis=0, keepdims=True), 1e-30)
            send_q[level][t, i] = jnp.round(x * (STEPS / peak)).astype(jnp.int32).astype(jnp.int16)
            send_s[level][t, i] = jnp.broadcast_to(peak * (1.0 / STEPS), (8, width))
        for copy in z_copies(level, t):
            copy.start()
        for i in range(R >> (level + 1)):
            keep[level][t, i] = get(2 * i + bit)

    def arrived(level, t):
        for copy in z_copies(level, t):
            copy.wait_recv()

        def get(i):
            scale = recv_s[level][t, i][0:1, :]
            coded = recv_q[level][t, i].astype(jnp.int32).astype(jnp.float32)
            return keep[level][t, i] + coded * scale

        return get

    def columns(who):
        return pl.ds(pl.multiple_of(who * width, width), width)

    def deliver(t):
        h, tile = t // tiles, t % tiles
        total = arrived(levels - 1, t)(0)
        fin[t] = total.astype(jnp.bfloat16).reshape(C // 2, share, width)
        for j in range(C // 2):
            target = 2 * j + h

            @pl.when(target != c)
            def _():
                pltpu.make_async_remote_copy(
                    src_ref=fin.at[t, j],
                    dst_ref=out_ref.at[tile, :, columns(c)],
                    send_sem=out_send,
                    recv_sem=out_recv,
                    device_id=(r, target),
                    device_id_type=MESH,
                ).start()

            @pl.when(target == c)
            def _():
                pltpu.make_async_copy(
                    fin.at[t, j], out_ref.at[tile, :, columns(c)], out_recv
                ).start()

    def multiply(h, tile, t):
        for j in range(per):
            block = order_ref[0, tile * per + j]
            pair_tile = order_ref[1, tile * per + j]
            left = held[h][pair_tile].reshape(R * slab_rows, -1)
            part = jnp.dot(
                left, blocks_vmem[block], preferred_element_type=jnp.float32
            ).reshape(R, slab_rows, width)
            if j == 0:
                acc[...] = part
            else:
                acc[...] += part
        exchange(0, t, lambda i: acc[i])

    def later(t):
        for level in range(1, levels):
            back = t - LAG * level

            @pl.when(jnp.logical_and(back >= 0, back < chunks))
            def _():
                exchange(level, back, arrived(level - 1, back))

        last = t - LAG * levels

        @pl.when(jnp.logical_and(last >= 0, last < chunks))
        def _():
            deliver(last)

    def run(h, lower, upper):
        @pl.loop(lower, upper)
        def _(tile):
            t = h * tiles + tile
            multiply(h, tile, t)
            later(t)

    send_own(0)
    pass_near(0)
    send_own(1)
    pass_far(0)
    finish(0)
    blocks_copy.wait()
    run(0, 0, tiles // 2)
    pass_near(1)
    run(0, tiles // 2, tiles)
    pass_far(1)
    finish(1)
    run(1, 0, tiles)

    @pl.loop(chunks, chunks + LAG * levels)
    def _(t):
        later(t)

    finish_sends(0)
    finish_sends(1)
    for level in range(levels):

        @pl.loop(0, chunks)
        def _(t):
            for copy in z_copies(level, t):
                copy.wait_send()

    rest_of = out_ref.at[:, :, pl.ds(0, (C - 1) * width)]
    pltpu.make_async_copy(rest_of, rest_of, out_send).wait()
    pltpu.make_async_copy(out_ref, out_ref, out_recv).wait()


def on_device(R, C, amplitudes, integrals, blocks):
    pairs, tiles, inner = amplitudes.shape
    count, _, width = integrals.shape
    per = count // tiles
    levels = R.bit_length() - 1
    share = pairs * C // (R * C)
    groups = pairs // share
    chunks = 2 * tiles
    slab_rows = pairs * C // R // 2

    key = blocks[:, 1] * count + jnp.arange(count, dtype=jnp.int32)
    rank = jnp.sum((key[:, None] > key[None, :]).astype(jnp.int32), axis=1)
    at = rank[:, None] == jnp.arange(count, dtype=jnp.int32)[None, :]
    both = jnp.stack([jnp.arange(count, dtype=jnp.int32), blocks[:, 0]], axis=0)
    order = jnp.sum(jnp.where(at[None], both[:, :, None], 0), axis=1)

    halves = amplitudes.reshape(groups // 2, 2, share, tiles, inner)
    halves = halves.transpose(1, 3, 0, 2, 4).reshape(2, tiles, pairs // 2, inner)

    held = pltpu.VMEM((tiles, C, pairs // 2, inner), jnp.bfloat16)
    parts = [R >> (level + 1) for level in range(levels)]
    coded = [pltpu.VMEM((chunks, n, slab_rows, width), jnp.int16) for n in parts]
    scales = [pltpu.VMEM((chunks, n, 8, width), jnp.float32) for n in parts]
    dma = pltpu.SemaphoreType.DMA
    out = pl.pallas_call(
        functools.partial(kernel, (R, C, tiles, per)),
        out_shape=jax.ShapeDtypeStruct((tiles, share, C * width), jnp.bfloat16),
        in_specs=[
            pl.BlockSpec(memory_space=pltpu.SMEM),
            pl.BlockSpec(memory_space=pl.ANY),
            pl.BlockSpec(memory_space=pl.ANY),
        ],
        out_specs=pl.BlockSpec(memory_space=pltpu.VMEM),
        scratch_shapes=[
            held,
            held,
            pltpu.VMEM(integrals.shape, jnp.bfloat16),
            pltpu.VMEM((R, slab_rows, width), jnp.float32),
            pltpu.VMEM((chunks, C // 2, share, width), jnp.bfloat16),
        ]
        + [pltpu.VMEM((chunks, n, slab_rows, width), jnp.float32) for n in parts]
        + coded
        + coded
        + scales
        + scales
        + [
            dma,
            dma((2,)),
            dma((2, 2, C)),
            dma((2, 2, C)),
            dma((levels, chunks)),
            dma((levels, chunks)),
            dma((levels, chunks)),
            dma((levels, chunks)),
            dma,
            dma,
        ],
        compiler_params=pltpu.CompilerParams(
            collective_id=0, has_side_effects=True, vmem_limit_bytes=67043328
        ),
    )(order, halves, integrals)
    return out.transpose(1, 0, 2)


def solution(mesh):
    return jax.shard_map(
        functools.partial(on_device, mesh.shape["row"], mesh.shape["col"]),
        mesh=mesh,
        in_specs=(P("col", None, "row"), P(None, "row", "col"), P()),
        out_specs=P(("row", "col"), None, None),
        check_vma=False,
    )
```

time: 345 us -> 130 us (0.38)
  waiting for transfers between devices: 158 us -> 0 us
  Pallas kernels: 0 us -> 120 us
  local copies, waits for them, and re-layouts: 95.3 us -> 5.55 us
  matrix products: 55.1 us -> 0 us
  blocking collectives: 18.8 us -> 0 us
  between operations: 13.5 us -> 0.02 us
    reduce_scatter x1 -> x0, waiting for transfers between devices: 145 us -> none  [on_device(): lax.psum_scatter(contract(gathered, integrals, sorted_rows, sorted_blocks...]
    pallas_call x0 -> x1, Pallas kernels: none -> 120 us  [on_device(): pl.pallas_call(functools.partial(kernel, (R, C, tiles, per)), out_shape=j...]
    gather x17 -> x0, local copies, waits for them, and re-layouts: 90.1 us -> none  [the longest x8 49.3 us: contract(): jnp.take(panel_rows, sorted_rows[lower:lower + per_column], axis=1)]
    dot_general x8 -> x0, matrix products: 55.1 us -> none  [contract(): jnp.dot(left_rows, right_cols, preferred_element_type=jnp.float32)]
    all_to_all x1 -> x0, blocking collectives: 18.8 us -> none  [on_device(): lax.all_to_all(summed.astype(jnp.bfloat16), 'col', split_axis=0, concat_a...]
    all_gather x1 -> x0, waiting for transfers between devices: 13.6 us -> none  [on_device(): gathered = lax.all_gather(amplitudes, 'col', axis=0, tiled=True)]
  transfers between devices with their start and end apart: 2 -> 0, of which waited for: 2 -> 0; matrix products, arithmetic and copies ran while one was open for 13% -> 0% of each run, Pallas kernels for 0% -> 0%
where the time goes in v1:
time: 130 us; the launch traced here: 128 us
  Pallas kernels  120 us (92%)
  local copies, waits for them, and re-layouts  5.55 us (4%)
  other arithmetic  2.39 us (2%)
    pallas_call x1, Pallas kernels, on_device(): pl.pallas_call(functools.partial(kernel, (R, C, tiles, per)), out_shape=j...  120 us
    transpose x1, local copies, waits for them, and re-layouts, on_device(): return out.transpose(1, 0, 2)  2.78 us
    reshape x1, local copies, waits for them, and re-layouts, on_device(): halves = amplitudes.reshape(groups // 2, 2, share, tiles, inner)  2.77 us

profile of v1, /device:TPU:0, one launch (start us, length us, event | category | flops | bytes accessed | tf_op | source)
XLA Modules:
  0.0 128.0 jit_solution(18343106319803738499)
XLA Ops:
  0.0 0.7 bitcast_add_fusion
  0.7 0.8 add_bitcast_fusion
  1.4 0.2 convert_reduce_fusion
  1.6 0.1 iota_compare_fusion
  1.7 0.7 select_reduce_fusion.order_ref
  2.4 2.8 %copy.6 = bf16[2,2,16,8,1024]{4,2,0,3,1:T(8,128)(2,1)} copy(bf16[2,2,16,8,1024]{4,3,2,1,0:T(8,128)(2,1)} %bitcast.13) | data formatting | bytes 2097152 | tf_op jit(solution)/shard_map/reshape | solution.py:294
  5.2 120.1 %shard_map.37 = bf16[8,16,4096]{2,1,0:T(8,128)(2,1)} custom-call(s32[2,32]{1,0:T(2,128)} %select_reduce_fusion.order_ref, bf16[2,8,32,1024]{3,2,1,0:T(8,128)(2,1)} %bitcast.12, bf16[32,1024,512]{2,1,0:T(8,128)(2,1)} %int_ref.1), custom_call_target="tpu_custom_call" | custom-call | tf_op jit(solution)/shard_map/pallas_call | solution.py:302
  125.3 2.8 %copy.7 = bf16[16,8,4096]{2,1,0:T(8,128)(2,1)} copy(bf16[16,8,4096]{2,0,1:T(8,128)(2,1)} %bitcast.11) | data formatting | bytes 2097152 | tf_op jit(solution)/shard_map/transpose | solution.py:339
  (2 shorter events, 0.0 us)
